TPU v7x, 512 devices: a whole 4x8x8 slice. The times are simulated.
512 devices in a mesh: dp: 16 (over z, core), seq: 32 (over x, y).
Axes of the slice: x: 4, y: 8, z: 8, core: 2. Of those that a mesh axis runs over, the one named last changes fastest.
Arguments:
- inputs: bfloat16 [16, 4096, 4096], P('dp', 'seq'), may hold values from -6 to 6
- out_grads: bfloat16 [16, 4096, 14336], P('dp', 'seq'), may hold values from -6 to 6
- valid: int32 [16, 4096], P('dp', 'seq'), may hold values 0 or 1
- doc_blocks: int32 [16, 4], P('dp'), may hold values from 1 to 16, 32 in all within a row
- doc_ids: int32 [64], replicated, may hold values from 0 to 63, each once
- proj_in: bfloat16 [4096, 64], P('seq'), may hold values from -0.09375 to 0.09375
- proj_out: bfloat16 [14336, 64], P('seq'), may hold values from -0.046875 to 0.046875
- test_grads: bfloat16 [1024, 4096], P('seq'), may hold values from -192 to 192
Outputs:
- scores: float32 [64, 1024], P(None, 'seq')
Inputs may be any that keep to these rules, and one draw needn't show every extreme that they name: `doc_blocks`: each group's lengths sum to 32; the largest is 16 in every group. `doc_ids`: every document number appears once.
All inputs are finite; a program needn't handle non-finite values. No bound on the sum of `valid` on one device may be relied on, other than what follows from the above.
Results may differ from a plain program's by a relative error of at most 0.0003.
Values may be sent and summed in bfloat16 or wider, within the bound.
A program may use at most 64 MiB of HBM per device.

v0:
```python
import jax
import jax.numpy as jnp
from jax import lax
from jax.sharding import PartitionSpec as P

PROJ_OUT = 64
FEAT = 4096
BLOCK = 128
DOC_GRP = 4


def per_device(inputs, out_grads, valid, doc_blocks, doc_ids, proj_in, proj_out, test_grads):
    tokens = inputs[0]
    outgrad = out_grads[0]
    slots = tokens.shape[0]
    columns = tokens
    px = jnp.dot(
        columns,
        lax.all_gather(proj_in, "seq", axis=0, tiled=True),
        preferred_element_type=jnp.float32,
    )
    columns = outgrad
    pg = jnp.dot(
        columns,
        lax.all_gather(proj_out, "seq", axis=0, tiled=True),
        preferred_element_type=jnp.float32,
    )
    ends = jnp.cumsum(doc_blocks[0])
    position = lax.axis_index("seq") * slots + jnp.arange(slots, dtype=jnp.int32)
    blk = position // BLOCK
    owner = jnp.sum((blk[:, None] >= ends[None, :]).astype(jnp.int32), axis=1)
    onehot = (
        (owner[:, None] == jnp.arange(DOC_GRP, dtype=jnp.int32)[None, :]) & (valid[0][:, None] == 1)
    ).astype(jnp.float32)
    weighted = (onehot[:, :, None] * pg[:, None, :]).reshape(slots, DOC_GRP * PROJ_OUT)
    partial_grads = jnp.dot(weighted.T, px, precision=lax.Precision.HIGHEST).reshape(DOC_GRP, FEAT)
    ndocs = DOC_GRP * lax.axis_size("dp")
    group_grads = lax.psum(partial_grads, "seq")
    doc_grads = lax.all_gather(group_grads, "dp", axis=0, tiled=True)
    gram = jnp.dot(doc_grads, doc_grads.T, precision=lax.Precision.HIGHEST)
    cross = jnp.dot(doc_grads, test_grads.astype(jnp.float32).T, precision=lax.Precision.HIGHEST)
    damp = 0.1 * jnp.trace(gram) / ndocs
    matrix = gram / ndocs + damp * jnp.eye(ndocs, dtype=jnp.float32)
    factor = jnp.linalg.cholesky(matrix)
    middle = lax.linalg.triangular_solve(factor, cross, left_side=True, lower=True)
    solved = lax.linalg.triangular_solve(
        factor, middle, left_side=True, lower=True, transpose_a=True
    )
    placing = (doc_ids[None, :] == jnp.arange(ndocs, dtype=jnp.int32)[:, None]).astype(jnp.float32)
    return jnp.dot(placing, solved, precision=lax.Precision.HIGHEST)


def solution(mesh):
    in_specs = (
        P("dp", "seq", None),
        P("dp", "seq", None),
        P("dp", "seq"),
        P("dp", None),
        P(),
        P("seq", None),
        P("seq", None),
        P("seq", None),
    )
    out_specs = P(None, "seq")
    return jax.shard_map(
        per_device, mesh=mesh, in_specs=in_specs, out_specs=out_specs, check_vma=False
    )
```

profile of v0, /device:TPU:1, one launch (start us, length us, event | category | flops | bytes accessed | tf_op | source)
XLA Modules:
  0.0 325.9 jit_solution(14330074124522014039)
XLA Ops:
  6.5 0.7 all-gather.5.cloned.1.call-update
  7.3 0.0 all-reduce.2.cloned.1.call-start
  7.3 0.8 reduce-window.8
  8.1 0.1 convert_reduce_fusion
  8.2 41.4 %all_gather.10 = bf16[4096,64]{0,1:T(8,128)(2,1)S(1)} all-gather(bf16[128,64]{0,1:T(8,128)(2,1)} %param.13), channel_id=1, replica_groups=mesh['dp'=16,'seq'=32] {'seq'}, dimensions={0}, use_global_device_ids=true | all-gather | bytes 540672 | tf_op jit(solution)/shard_map/all_gather | solution.py:19
  49.6 0.7 compare_bitcast_fusion
  50.3 0.5 fusion.2
  50.8 44.7 %all-gather.5.cloned.1.call-done = bf16[32,448,64]{1,2,0:T(8,128)(2,1)} async-done(((bf16[1,448,64]{1,2,0:T(8,128)(2,1)}), bf16[32,448,64]{1,2,0:T(8,128)(2,1)}) %all-gather.5.cloned.1.call-update) | async-done | bytes 1835024 | tf_op jit(solution)/shard_map/all_gather | solution.py:25
  95.6 2.8 copy.20
  98.3 3.4 %reshape.113 = bf16[14336,64]{0,1:T(8,128)(2,1)} reshape(bf16[32,448,64]{1,0,2:T(8,128)(2,1)S(1)} %copy.20) | data formatting | bytes 3670016
  101.7 4.0 %fusion = f32[128,64]{0,1:T(8,128)S(1)} fusion(bf16[14336,64]{0,1:T(8,128)(2,1)} %reshape.113, bf16[1,128,14336]{2,1,0:T(8,128)(2,1)} %param.9), kind=kOutput, calls=%fused_computation | convolution fusion | flops 234881024 | bytes 5537792 | tf_op jit(solution)/shard_map/dot_general | solution.py:23
  105.7 0.3 fusion.15
  106.0 0.7 reshape.111
  106.7 0.0 all-reduce.2.cloned.1.call-update
  106.7 0.0 all-gather.7.cloned.1.call-start
  106.8 147.6 %all-reduce.2.cloned.1.call-done = f32[4,4096]{1,0:T(4,128)} async-done(((f32[4,4096]{1,0:T(4,128)}), f32[4,4096]{1,0:T(4,128)}) %all-reduce.2.cloned.1.call-update) | async-done | bytes 65552 | tf_op jit(solution)/shard_map/psum | solution.py:38
  254.4 0.0 all-gather.7.cloned.1.call-update
  254.4 47.1 %all-gather.7.cloned.1.call-done = f32[16,4,4096]{2,1,0:T(4,128)} async-done(((f32[1,4,4096]{2,1,0:T(4,128)}), f32[16,4,4096]{2,1,0:T(4,128)}) %all-gather.7.cloned.1.call-update) | async-done | bytes 1048592 | tf_op jit(solution)/shard_map/all_gather | solution.py:39
  301.5 1.6 reshape.115
  303.1 1.6 select_reduce_fusion.1
  304.7 0.1 copy.22
  304.8 0.1 copy.23
  305.6 5.8 %cholesky.17 = f32[64,64]{1,0:T(8,128)S(1)} custom-call(f32[64,64]{1,0:T(8,128)S(1)} %fusion.10), custom_call_target="Cholesky" | custom-call | tf_op jit(solution)/shard_map/jit(cholesky)/cholesky | solution.py:44
  311.4 0.6 compare_reduce_fusion
  312.1 0.7 fusion.4
  312.8 4.9 %custom-call.8 = f32[1,64,64]{1,2,0:T(8,128)S(1)} custom-call(f32[1,64,64]{2,1,0:T(8,128)S(1)} %fusion.4), custom_call_target="InvertDiagBlocksLowerTriangular" | custom-call | tf_op jit(solution)/shard_map/triangular_solve | solution.py:46
  317.6 0.0 copy-done.1
  317.7 0.6 fusion.16
  318.3 0.1 fusion.7
  318.4 0.2 fusion.5
  318.6 0.0 copy-done.2
  318.6 0.8 fusion.11
  (11 shorter events, 0.1 us)
Async XLA Ops:
  6.5 43.8 %copy-start = (bf16[1,128,4096]{2,1,0:T(8,128)(2,1)S(1)}, bf16[1,128,4096]{2,1,0:T(8,128)(2,1)}, u32[]{:S(2)}) copy-start(bf16[1,128,4096]{2,1,0:T(8,128)(2,1)} %param.8) | copy-start | bytes 3145732
  6.5 89.0 %all-gather.5.cloned.1.call-start = ((), (), s32[]{:S(2)}) async-start(), calls=%async_computation.1 | async-start | bytes 2162688 | tf_op jit(solution)/shard_map/all_gather | solution.py:25
  7.3 247.2 %all-reduce.2.cloned.1.call-start = ((), (), s32[]{:S(2)}) async-start(), calls=%async_computation | async-start | bytes 131072 | tf_op jit(solution)/shard_map/psum | solution.py:38
  106.7 194.8 %all-gather.7.cloned.1.call-start = ((), (), s32[]{:S(2)}) async-start(), calls=%async_computation.2 | async-start | bytes 1114112 | tf_op jit(solution)/shard_map/all_gather | solution.py:39
  254.4 63.2 %copy-start.1 = (bf16[32,4096]{1,0:T(8,128)(2,1)S(1)}, bf16[32,4096]{1,0:T(8,128)(2,1)}, u32[]{:S(2)}) copy-start(bf16[32,4096]{1,0:T(8,128)(2,1)} %param.15) | copy-start | bytes 786436
  303.1 15.5 %copy-start.2 = (s32[64]{0:T(128)S(1)}, s32[64]{0:T(128)}, u32[]{:S(2)}) copy-start(s32[64]{0:T(128)} %param.12) | copy-start | bytes 772
Sparse Core Ops, SparseCore 0:
  10.5 84.9 all-gather.4
  106.8 147.5 all-reduce.1
  256.5 44.9 all-gather.6
where the time goes:
time: 326 us
  waiting for transfers between devices  240 us (74%)
  blocking collectives  41.4 us (13%)
  between operations  13.9 us (4%)
  other arithmetic  13.7 us (4%)
  local copies, waits for them, and re-layouts  8.61 us (3%)
  matrix products  8 us (2%)
    psum x1, waiting for transfers between devices, per_device(): group_grads = lax.psum(partial_grads, 'seq')  148 us
    all_gather x1, waiting for transfers between devices, per_device(): doc_grads = lax.all_gather(group_grads, 'dp', axis=0, tiled=True)  47.1 us
    all_gather x1, waiting for transfers between devices, per_device(): lax.all_gather(proj_out, 'seq', axis=0, tiled=True)  44.7 us
    all_gather x1, blocking collectives, per_device(): lax.all_gather(proj_in, 'seq', axis=0, tiled=True)  41.4 us
  transfers between devices with their start and end apart: 3, of which 3 were waited for; matrix products, arithmetic and copies ran while one was open for 1% of the time, Pallas kernels for 0%

commit v1 on v0

--- a/solution.py
+++ b/solution.py
@@ -9,16 +9,20 @@
 DOC_GRP = 4
 
 
+def gather_from_all(array, axis, dim):
+    size = lax.axis_size(axis)
+    repeats = [size if d == dim else 1 for d in range(array.ndim)]
+    return lax.all_to_all(
+        jnp.tile(array, repeats), axis, split_axis=dim, concat_axis=dim, tiled=True
+    )
+
+
 def per_device(inputs, out_grads, valid, doc_blocks, doc_ids, proj_in, proj_out, test_grads):
     tokens = inputs[0]
     outgrad = out_grads[0]
     slots = tokens.shape[0]
     columns = tokens
-    px = jnp.dot(
-        columns,
-        lax.all_gather(proj_in, "seq", axis=0, tiled=True),
-        preferred_element_type=jnp.float32,
-    )
+    px = jnp.dot(columns, gather_from_all(proj_in, "seq", 0), preferred_element_type=jnp.float32)
     columns = outgrad
     pg = jnp.dot(
         columns,

time: 326 us -> 326 us (level)
  blocking collectives: 41.4 us -> 0 us
  waiting for transfers between devices: 240 us -> 270 us
  starting transfers between devices: 0.08 us -> 10.6 us
    all_gather x1 -> x0, blocking collectives: 41.4 us -> none  [per_device(): lax.all_gather(proj_in, 'seq', axis=0, tiled=True)]
    all_gather x1, waiting for transfers between devices: 44.7 us -> 61.4 us  [per_device(): lax.all_gather(proj_out, 'seq', axis=0, tiled=True)]
    all_to_all x0 -> x1, waiting for transfers between devices: none -> 12.7 us  [gather_from_all(): lax.all_to_all(jnp.tile(array, repeats), axis, split_axis=dim, concat_axi...]
    all_to_all x0 -> x1, starting transfers between devices: none -> 10.5 us  [gather_from_all(): lax.all_to_all(jnp.tile(array, repeats), axis, split_axis=dim, concat_axi...]
  transfers between devices with their start and end apart: 3 -> 4, of which waited for: 3 -> 4; matrix products, arithmetic and copies ran while one was open for 1% -> 1% of each run, Pallas kernels for 0% -> 0%
where the time goes in v1:
time: 326 us
  waiting for transfers between devices  270 us (83%)
  between operations  13.9 us (4%)
  other arithmetic  13.7 us (4%)
  starting transfers between devices  10.6 us (3%)
  local copies, waits for them, and re-layouts  10.2 us (3%)
  matrix products  7.98 us (2%)
    psum x1, waiting for transfers between devices, per_device(): group_grads = lax.psum(partial_grads, 'seq')  148 us
    all_gather x1, waiting for transfers between devices, per_device(): lax.all_gather(proj_out, 'seq', axis=0, tiled=True)  61.4 us
    all_gather x1, waiting for transfers between devices, per_device(): doc_grads = lax.all_gather(group_grads, 'dp', axis=0, tiled=True)  47.1 us
    all_to_all x1, waiting for transfers between devices, gather_from_all(): lax.all_to_all(jnp.tile(array, repeats), axis, split_axis=dim, concat_axi...  12.7 us
    all_to_all x1, starting transfers between devices, gather_from_all(): lax.all_to_all(jnp.tile(array, repeats), axis, split_axis=dim, concat_axi...  10.5 us
  transfers between devices with their start and end apart: 4, of which 4 were waited for; matrix products, arithmetic and copies ran while one was open for 1% of the time, Pallas kernels for 0%

profile of v1, /device:TPU:1, one launch (start us, length us, event | category | flops | bytes accessed | tf_op | source)
XLA Modules:
  0.0 325.9 jit_solution(4094946442630826706)
XLA Ops:
  6.5 0.7 all-gather.5.cloned.1.call-update
  7.3 1.6 tile.2
  8.9 10.5 %all-to-all-start = ((bf16[32,128,64]{1,2,0:T(8,128)(2,1)}), bf16[32,128,64]{1,2,0:T(8,128)(2,1)S(1)}, u32[]{:S(2)}, u32[]{:S(2)}) async-start(bf16[32,128,64]{1,2,0:T(8,128)(2,1)} %tile.2), calls=%async_computation | async-start | bytes 1048576 | tf_op jit(solution)/shard_map/all_to_all | solution.py:15
  19.4 0.0 all-reduce.2.cloned.1.call-start
  19.5 0.8 reduce-window.8
  20.3 0.1 convert_reduce_fusion
  20.4 0.7 compare_bitcast_fusion
  21.0 12.7 %all-to-all-done = bf16[32,128,64]{1,2,0:T(8,128)(2,1)S(1)} async-done(((bf16[32,128,64]{1,2,0:T(8,128)(2,1)}), bf16[32,128,64]{1,2,0:T(8,128)(2,1)S(1)}, u32[]{:S(2)}, u32[]{:S(2)}) %all-to-all-start) | async-done | bytes 524320 | tf_op jit(solution)/shard_map/all_to_all | solution.py:15
  33.7 0.5 fusion.2
  34.2 61.4 %all-gather.5.cloned.1.call-done = bf16[32,448,64]{1,2,0:T(8,128)(2,1)} async-done(((bf16[1,448,64]{1,2,0:T(8,128)(2,1)}), bf16[32,448,64]{1,2,0:T(8,128)(2,1)}) %all-gather.5.cloned.1.call-update) | async-done | bytes 1835024 | tf_op jit(solution)/shard_map/all_gather | solution.py:29
  95.6 2.8 copy.27
  98.3 3.4 %reshape.120 = bf16[14336,64]{0,1:T(8,128)(2,1)} reshape(bf16[32,448,64]{1,0,2:T(8,128)(2,1)S(1)} %copy.27) | data formatting | bytes 3670016
  101.7 4.0 %fusion = f32[128,64]{0,1:T(8,128)S(1)} fusion(bf16[14336,64]{0,1:T(8,128)(2,1)} %reshape.120, bf16[1,128,14336]{2,1,0:T(8,128)(2,1)} %param.9), kind=kOutput, calls=%fused_computation | convolution fusion | flops 234881024 | bytes 5537792 | tf_op jit(solution)/shard_map/dot_general | solution.py:27
  105.7 0.3 fusion.17
  106.0 0.7 reshape.118
  106.7 0.0 all-reduce.2.cloned.1.call-update
  106.8 0.0 all-gather.7.cloned.1.call-start
  106.8 147.6 %all-reduce.2.cloned.1.call-done = f32[4,4096]{1,0:T(4,128)} async-done(((f32[4,4096]{1,0:T(4,128)}), f32[4,4096]{1,0:T(4,128)}) %all-reduce.2.cloned.1.call-update) | async-done | bytes 65552 | tf_op jit(solution)/shard_map/psum | solution.py:42
  254.4 0.0 all-gather.7.cloned.1.call-update
  254.5 47.1 %all-gather.7.cloned.1.call-done = f32[16,4,4096]{2,1,0:T(4,128)} async-done(((f32[1,4,4096]{2,1,0:T(4,128)}), f32[16,4,4096]{2,1,0:T(4,128)}) %all-gather.7.cloned.1.call-update) | async-done | bytes 1048592 | tf_op jit(solution)/shard_map/all_gather | solution.py:43
  301.6 1.6 reshape.122
  303.2 1.6 select_reduce_fusion.1
  304.7 0.1 copy.30
  304.8 0.1 copy.31
  305.6 5.8 %cholesky.17 = f32[64,64]{1,0:T(8,128)S(1)} custom-call(f32[64,64]{1,0:T(8,128)S(1)} %fusion.12), custom_call_target="Cholesky" | custom-call | tf_op jit(solution)/shard_map/jit(cholesky)/cholesky | solution.py:48
  311.5 0.6 compare_reduce_fusion
  312.1 0.7 fusion.6
  312.8 4.9 %custom-call.8 = f32[1,64,64]{1,2,0:T(8,128)S(1)} custom-call(f32[1,64,64]{2,1,0:T(8,128)S(1)} %fusion.6), custom_call_target="InvertDiagBlocksLowerTriangular" | custom-call | tf_op jit(solution)/shard_map/triangular_solve | solution.py:50
  317.7 0.6 fusion.18
  318.3 0.1 fusion.9
  318.5 0.2 fusion.7
  318.7 0.8 fusion.13
  (13 shorter events, 0.1 us)
Async XLA Ops:
  6.5 27.2 %copy-start = (bf16[1,128,4096]{2,1,0:T(8,128)(2,1)S(1)}, bf16[1,128,4096]{2,1,0:T(8,128)(2,1)}, u32[]{:S(2)}) copy-start(bf16[1,128,4096]{2,1,0:T(8,128)(2,1)} %param.8) | copy-start | bytes 3145732
  6.5 89.1 %all-gather.5.cloned.1.call-start = ((), (), s32[]{:S(2)}) async-start(), calls=%async_computation.2 | async-start | bytes 2162688 | tf_op jit(solution)/shard_map/all_gather | solution.py:29
  8.9 24.8 %all-to-all-start = ((bf16[32,128,64]{1,2,0:T(8,128)(2,1)}), bf16[32,128,64]{1,2,0:T(8,128)(2,1)S(1)}, u32[]{:S(2)}, u32[]{:S(2)}) async-start(bf16[32,128,64]{1,2,0:T(8,128)(2,1)} %tile.2), calls=%async_computation | async-start | bytes 1048576 | tf_op jit(solution)/shard_map/all_to_all | solution.py:15
  19.4 235.0 %all-reduce.2.cloned.1.call-start = ((), (), s32[]{:S(2)}) async-start(), calls=%async_computation.1 | async-start | bytes 131072 | tf_op jit(solution)/shard_map/psum | solution.py:42
  106.8 194.8 %all-gather.7.cloned.1.call-start = ((), (), s32[]{:S(2)}) async-start(), calls=%async_computation.3 | async-start | bytes 1114112 | tf_op jit(solution)/shard_map/all_gather | solution.py:43
  254.5 63.2 %copy-start.1 = (bf16[32,4096]{1,0:T(8,128)(2,1)S(1)}, bf16[32,4096]{1,0:T(8,128)(2,1)}, u32[]{:S(2)}) copy-start(bf16[32,4096]{1,0:T(8,128)(2,1)} %param.15) | copy-start | bytes 786436
  303.2 15.5 %copy-start.2 = (s32[64]{0:T(128)S(1)}, s32[64]{0:T(128)}, u32[]{:S(2)}) copy-start(s32[64]{0:T(128)} %param.12) | copy-start | bytes 772
Sparse Core Ops, SparseCore 0:
  10.5 85.0 all-gather.4
  106.9 147.5 all-reduce.1
  256.6 44.9 all-gather.6

commit v2 on v0

--- a/solution.py
+++ b/solution.py
@@ -35,7 +35,7 @@
     weighted = (onehot[:, :, None] * pg[:, None, :]).reshape(slots, DOC_GRP * PROJ_OUT)
     partial_grads = jnp.dot(weighted.T, px, precision=lax.Precision.HIGHEST).reshape(DOC_GRP, FEAT)
     ndocs = DOC_GRP * lax.axis_size("dp")
-    group_grads = lax.psum(partial_grads, "seq")
+    group_grads = jnp.sum(lax.all_gather(partial_grads, "seq"), axis=0)
     doc_grads = lax.all_gather(group_grads, "dp", axis=0, tiled=True)
     gram = jnp.dot(doc_grads, doc_grads.T, precision=lax.Precision.HIGHEST)
     cross = jnp.dot(doc_grads, test_grads.astype(jnp.float32).T, precision=lax.Precision.HIGHEST)

time: 326 us -> 259 us (0.79)
  waiting for transfers between devices: 240 us -> 170 us
    psum x1 -> x0, waiting for transfers between devices: 148 us -> none  [per_device(): group_grads = lax.psum(partial_grads, 'seq')]
    all_gather x0 -> x1, waiting for transfers between devices: none -> 80.9 us  [per_device(): group_grads = jnp.sum(lax.all_gather(partial_grads, 'seq'), axis=0)]
    all_gather x1, waiting for transfers between devices: 47.1 us -> 43.7 us  [per_device(): doc_grads = lax.all_gather(group_grads, 'dp', axis=0, tiled=True)]
where the time goes in v2:
time: 259 us; the launch traced here: 258 us
  waiting for transfers between devices  170 us (66%)
  blocking collectives  41.4 us (16%)
  other arithmetic  16.2 us (6%)
  between operations  13.9 us (5%)
  local copies, waits for them, and re-layouts  8.61 us (3%)
  matrix products  8 us (3%)
    all_gather x1, waiting for transfers between devices, per_device(): group_grads = jnp.sum(lax.all_gather(partial_grads, 'seq'), axis=0)  80.9 us
    all_gather x1, waiting for transfers between devices, per_device(): lax.all_gather(proj_out, 'seq', axis=0, tiled=True)  44.7 us
    all_gather x1, waiting for transfers between devices, per_device(): doc_grads = lax.all_gather(group_grads, 'dp', axis=0, tiled=True)  43.7 us
    all_gather x1, blocking collectives, per_device(): lax.all_gather(proj_in, 'seq', axis=0, tiled=True)  41.4 us
    another operation x3, other arithmetic, per_device(): factor = jnp.linalg.cholesky(matrix)  6.52 us
    another operation x2, other arithmetic, per_device(): lax.linalg.triangular_solve(factor, middle, left_side=True, lower=True, t...  5.55 us
  transfers between devices with their start and end apart: 3, of which 3 were waited for; matrix products, arithmetic and copies ran while one was open for 1% of the time, Pallas kernels for 0%

profile of v2, /device:TPU:1, one launch (start us, length us, event | category | flops | bytes accessed | tf_op | source)
XLA Modules:
  0.0 258.3 jit_solution(12958160068024231276)
XLA Ops:
  6.5 0.7 all-gather.8.cloned.1.call-update
  7.3 0.0 all-gather.6.cloned.1.call-start
  7.3 0.8 reduce-window.8
  8.1 0.1 convert_reduce_fusion
  8.2 41.4 %all_gather.13 = bf16[4096,64]{0,1:T(8,128)(2,1)S(1)} all-gather(bf16[128,64]{0,1:T(8,128)(2,1)} %param.13), channel_id=1, replica_groups=mesh['dp'=16,'seq'=32] {'seq'}, dimensions={0}, use_global_device_ids=true | all-gather | bytes 540672 | tf_op jit(solution)/shard_map/all_gather | solution.py:19
  49.6 0.7 compare_bitcast_fusion
  50.3 0.5 fusion.2
  50.8 44.7 %all-gather.8.cloned.1.call-done = bf16[32,448,64]{1,2,0:T(8,128)(2,1)} async-done(((bf16[1,448,64]{1,2,0:T(8,128)(2,1)}), bf16[32,448,64]{1,2,0:T(8,128)(2,1)}) %all-gather.8.cloned.1.call-update) | async-done | bytes 1835024 | tf_op jit(solution)/shard_map/all_gather | solution.py:25
  95.6 2.8 %copy.20 = bf16[32,448,64]{1,0,2:T(8,128)(2,1)S(1)} copy(bf16[32,448,64]{1,2,0:T(8,128)(2,1)} %all-gather.8.cloned.1.call-done) | data formatting | bytes 3670016 | tf_op jit(solution)/shard_map/all_gather | solution.py:25
  98.3 3.4 %reshape.109 = bf16[14336,64]{0,1:T(8,128)(2,1)} reshape(bf16[32,448,64]{1,0,2:T(8,128)(2,1)S(1)} %copy.20) | data formatting | bytes 3670016
  101.7 4.0 %fusion = f32[128,64]{0,1:T(8,128)S(1)} fusion(bf16[14336,64]{0,1:T(8,128)(2,1)} %reshape.109, bf16[1,128,14336]{2,1,0:T(8,128)(2,1)} %param.9), kind=kOutput, calls=%fused_computation | convolution fusion | flops 234881024 | bytes 5537792 | tf_op jit(solution)/shard_map/dot_general | solution.py:23
  105.7 0.3 fusion.15
  106.0 0.7 all_gather_reshape.3
  106.7 0.0 all-gather.6.cloned.1.call-update
  106.7 0.0 all-gather.10.cloned.1.call-start
  106.8 80.9 %all-gather.6.cloned.1.call-done = f32[32,4,4096]{2,1,0:T(4,128)} async-done(((f32[1,4,4096]{2,1,0:T(4,128)}), f32[32,4,4096]{2,1,0:T(4,128)}) %all-gather.6.cloned.1.call-update) | async-done | bytes 2097168 | tf_op jit(solution)/shard_map/all_gather | solution.py:38
  187.6 2.5 reduce_sum.29
  190.2 0.0 all-gather.10.cloned.1.call-update
  190.2 43.7 %all-gather.10.cloned.1.call-done = f32[16,4,4096]{2,1,0:T(4,128)} async-done(((f32[1,4,4096]{2,1,0:T(4,128)}), f32[16,4,4096]{2,1,0:T(4,128)}) %all-gather.10.cloned.1.call-update) | async-done | bytes 1048592 | tf_op jit(solution)/shard_map/all_gather | solution.py:39
  233.9 1.6 reshape.111
  235.5 1.6 select_reduce_fusion.1
  237.1 0.1 copy.22
  237.2 0.1 copy.23
  237.9 5.8 %cholesky.17 = f32[64,64]{1,0:T(8,128)S(1)} custom-call(f32[64,64]{1,0:T(8,128)S(1)} %fusion.10), custom_call_target="Cholesky" | custom-call | tf_op jit(solution)/shard_map/jit(cholesky)/cholesky | solution.py:44
  243.8 0.6 compare_reduce_fusion
  244.4 0.7 fusion.4
  245.1 4.9 %custom-call.8 = f32[1,64,64]{1,2,0:T(8,128)S(1)} custom-call(f32[1,64,64]{2,1,0:T(8,128)S(1)} %fusion.4), custom_call_target="InvertDiagBlocksLowerTriangular" | custom-call | tf_op jit(solution)/shard_map/triangular_solve | solution.py:46
  250.0 0.0 copy-done.1
  250.0 0.6 fusion.16
  250.6 0.1 fusion.7
  250.8 0.2 fusion.5
  251.0 0.8 fusion.11
  (12 shorter events, 0.1 us)
Async XLA Ops:
  6.5 43.8 %copy-start = (bf16[1,128,4096]{2,1,0:T(8,128)(2,1)S(1)}, bf16[1,128,4096]{2,1,0:T(8,128)(2,1)}, u32[]{:S(2)}) copy-start(bf16[1,128,4096]{2,1,0:T(8,128)(2,1)} %param.8) | copy-start | bytes 3145732
  6.5 89.0 %all-gather.8.cloned.1.call-start = ((), (), s32[]{:S(2)}) async-start(), calls=%async_computation.1 | async-start | bytes 2162688 | tf_op jit(solution)/shard_map/all_gather | solution.py:25
  7.3 180.4 %all-gather.6.cloned.1.call-start = ((), (), s32[]{:S(2)}) async-start(), calls=%async_computation | async-start | bytes 2162688 | tf_op jit(solution)/shard_map/all_gather | solution.py:38
  106.7 127.2 %all-gather.10.cloned.1.call-start = ((), (), s32[]{:S(2)}) async-start(), calls=%async_computation.2 | async-start | bytes 1114112 | tf_op jit(solution)/shard_map/all_gather | solution.py:39
  190.2 59.8 %copy-start.1 = (bf16[32,4096]{1,0:T(8,128)(2,1)S(1)}, bf16[32,4096]{1,0:T(8,128)(2,1)}, u32[]{:S(2)}) copy-start(bf16[32,4096]{1,0:T(8,128)(2,1)} %param.15) | copy-start | bytes 786436
  235.5 15.5 %copy-start.2 = (s32[64]{0:T(128)S(1)}, s32[64]{0:T(128)}, u32[]{:S(2)}) copy-start(s32[64]{0:T(128)} %param.12) | copy-start | bytes 772
Sparse Core Ops, SparseCore 0:
  10.5 84.9 all-gather.7
  106.8 80.7 all-gather.5
  190.3 43.5 all-gather.9
